TPU v7x, 128 devices: a whole 4x4x4 slice. The times are simulated.
128 devices in a mesh: group: 8 (over x, core), sub: 16 (over z, y).
Axes of the slice: x: 4, y: 4, z: 4, core: 2. Of those that a mesh axis runs over, the one named last changes fastest.
Arguments:
- schur: bfloat16 [8, 16, 1024, 1024], P('group', 'sub'), as said below
- local_inverse: bfloat16 [8, 16, 1024, 1024], P('group', 'sub'), as said below
- rhs_parts: bfloat16 [8, 16, 1024, 128], P('group', 'sub'), may hold values from -6 to 6
- basis: bfloat16 [8, 16, 32, 1024], P('group', 'sub'), may hold values from -0.1875 to 0.1875
- coarse_map: int32 [8, 16, 32], P('group', 'sub'), may hold values from 0 to 1023
- coarse_inverse: bfloat16 [8, 1024, 1024], P('group', 'sub'), as said below
- shared_rows: int32 [8, 16, 2, 4, 256], P('group', 'sub'), may hold values from 0 to 1023, as said below
- shared_counts: int32 [8, 16, 4], P('group', 'sub'), may hold values from 0 to 256, as said below
Outputs:
- solution: float32 [8, 16, 1024, 128], P('group', 'sub')
- residual: float32 [8, 16, 1024, 128], P('group', 'sub')
Inputs may be any that keep to these rules, and one draw needn't show every extreme that they name: `schur`: each subdomain matrix is symmetric positive definite. `local_inverse`: each subdomain matrix is symmetric positive definite. `coarse_inverse`: each group's matrix is symmetric positive definite. `shared_rows`: own rows of direction d lie in rows d * 256 to (d + 1) * 256 - 1 and are distinct within a list; the own rows of direction 0 of (g, s) are the partner rows of direction 1 of (g, s + 1) and the reverse, likewise directions 2 and 3 between (g, s) and (g + 1, s); entries past the count are rows of the same block. `shared_counts`: the count of direction 0 of (g, s) equals the count of direction 1 of (g, s + 1), that of direction 2 of (g, s) the count of direction 3 of (g + 1, s); counts are 0 where no neighbour exists; some count equals 256.
All inputs are finite; a program needn't handle non-finite values.
Results may differ from a plain program's by a relative error of at most 0.014.
Values may be sent and summed in bfloat16 or wider, within the bound.
A program may use at most 64 MiB of HBM per device.

v0:
```python
import jax
import jax.numpy as jnp
from jax import lax
from jax.sharding import PartitionSpec as P

ITERS = 3


def extended(block, sides, width):
    for axis, dim in sides:
        count = lax.axis_size(axis)
        forward = [(i, i + 1) for i in range(count - 1)]
        backward = [(target, source) for source, target in forward]
        low = lax.ppermute(
            lax.slice_in_dim(block, block.shape[dim] - width, None, axis=dim), axis, forward
        )
        high = lax.ppermute(lax.slice_in_dim(block, 0, width, axis=dim), axis, backward)
        block = jnp.concatenate([low, block, high], axis=dim)
    return block


def pick_rows(tables, indices):
    return jax.vmap(jax.vmap(lambda source_block, rows_at: source_block[rows_at]))(tables, indices)


def add_rows(bases, indices, additions):

    def add_single(base_block, rows_at, extra):
        return base_block.at[rows_at.reshape(-1)].add(extra.reshape(-1, base_block.shape[-1]))

    return jax.vmap(jax.vmap(add_single))(bases, indices, additions)


def count_rows(indices, live_mask, rows_local):

    def count_single(rows_at, mask_rows):
        return (
            jnp.ones((rows_local,), jnp.float32).at[rows_at.reshape(-1)].add(mask_rows.reshape(-1))
        )

    return jax.vmap(jax.vmap(count_single))(indices, live_mask)


def assemble(blocks, own_rows, partner_rows, live_mask):
    padded = extended(blocks, (("group", 0), ("sub", 1)), 1)
    received = jnp.stack(
        [
            pick_rows(padded[1:2, 2:], partner_rows[:, :, 0]),
            pick_rows(padded[1:2, :-2], partner_rows[:, :, 1]),
            pick_rows(padded[2:3, 1:-1], partner_rows[:, :, 2]),
            pick_rows(padded[0:1, 1:-1], partner_rows[:, :, 3]),
        ],
        axis=2,
    )
    values = received * live_mask[..., None]
    return add_rows(blocks, own_rows, values)


def gram_matrix(left, right, weight):
    local_gram = jnp.einsum(
        "gsir,gsic->rc", left * weight[..., None], right, precision=lax.Precision.HIGHEST
    )
    return lax.psum(local_gram, ("group", "sub"))


def spd_solve(matrix, rhs_block):
    factor = jnp.linalg.cholesky(matrix)
    half = lax.linalg.triangular_solve(factor, rhs_block, left_side=True, lower=True)
    return lax.linalg.triangular_solve(factor, half, left_side=True, lower=True, transpose_a=True)


def contract(blocks, mixing):
    return jnp.einsum("gsir,rc->gsic", blocks, mixing, precision=lax.Precision.HIGHEST)


def shards(
    schur, local_inverse, rhs_parts, basis, coarse_map, coarse_inverse, shared_rows, shared_counts
):
    capacity = shared_rows.shape[-1]
    rows_local = rhs_parts.shape[2]
    columns = rhs_parts.shape[3]
    coarse_total = coarse_inverse.shape[2]
    live_mask = (jnp.arange(capacity, dtype=jnp.int32) < shared_counts[..., None]).astype(
        jnp.float32
    )
    own_rows = shared_rows[:, :, 0]
    partner_rows = shared_rows[:, :, 1]
    weight = 1.0 / count_rows(own_rows, live_mask, rows_local)
    selector = (
        coarse_map.reshape(-1)[:, None] == jnp.arange(coarse_total, dtype=jnp.int32)[None, :]
    ).astype(jnp.float32)
    selector_half = selector.astype(jnp.bfloat16)
    full_inverse = coarse_inverse[0]

    def precondition(resid):
        scaled = (weight[..., None] * resid).astype(jnp.bfloat16)
        local_part = jnp.einsum(
            "gsij,gsjr->gsir", local_inverse, scaled, preferred_element_type=jnp.float32
        )
        coarse_local = jnp.einsum(
            "gsmi,gsir->gsmr", basis, scaled, preferred_element_type=jnp.float32
        )
        contrib = jnp.dot(
            selector.T, coarse_local.reshape(-1, columns), precision=lax.Precision.HIGHEST
        )
        coarse_residual = lax.psum(contrib, "sub")
        coarse_rounded = coarse_residual.astype(jnp.bfloat16)
        row_values = jnp.dot(
            full_inverse, coarse_rounded, preferred_element_type=jnp.float32
        ).astype(jnp.bfloat16)
        coarse_values = lax.all_gather(row_values, "sub", axis=0, tiled=True)
        picked = (
            jnp.dot(selector_half, coarse_values, preferred_element_type=jnp.float32)
            .astype(jnp.bfloat16)
            .reshape(coarse_local.shape)
        )
        coarse_part = jnp.einsum(
            "gsmi,gsmr->gsir", basis, picked, preferred_element_type=jnp.float32
        )
        smoothed = weight[..., None] * (local_part + coarse_part)
        return assemble(smoothed, own_rows, partner_rows, live_mask)

    residual = assemble(rhs_parts.astype(jnp.float32), own_rows, partner_rows, live_mask)
    solution = jnp.zeros_like(residual)
    precond = precondition(residual)
    direction = precond
    inner = gram_matrix(precond, residual, weight)
    for iteration in range(ITERS):
        local_image = jnp.einsum(
            "gsij,gsjr->gsir",
            schur,
            direction.astype(jnp.bfloat16),
            preferred_element_type=jnp.float32,
        )
        image = assemble(local_image, own_rows, partner_rows, live_mask)
        curvature = gram_matrix(direction, image, weight)
        step_size = spd_solve(curvature, inner)
        solution = solution + contract(direction, step_size)
        residual = residual - contract(image, step_size)
        if iteration + 1 < ITERS:
            precond = precondition(residual)
            inner_next = gram_matrix(precond, residual, weight)
            conjugacy = spd_solve(inner, inner_next)
            direction = precond + contract(direction, conjugacy)
            inner = inner_next
    return (solution, residual)


def solution(mesh):
    placed = (
        P("group", "sub", None, None),
        P("group", "sub", None, None),
        P("group", "sub", None, None),
        P("group", "sub", None, None),
        P("group", "sub", None),
        P("group", "sub", None),
        P("group", "sub", None, None, None),
        P("group", "sub", None),
    )
    return jax.shard_map(
        shards,
        mesh=mesh,
        in_specs=placed,
        out_specs=(P("group", "sub", None, None), P("group", "sub", None, None)),
        check_vma=False,
    )
```

profile of v0, /device:TPU:1, one launch (start us, length us, event | category | flops | bytes accessed | tf_op | source)
XLA Modules:
  0.0 1686.3 jit_solution(6008829933205526659)
XLA Ops:
  44.1 14.3 collective-permute-done.3
  78.5 66.6 %all-reduce.19 = bf16[1024,128]{1,0:T(8,128)(2,1)} all-reduce(f32[1024,128]{1,0:T(8,128)S(1)} %fusion.81), channel_id=1, replica_groups=mesh['group'=8,'sub'=16] {'sub'}, use_global_device_ids=true, to_apply=%region_2.0 | all-reduce | flops 131072 | bytes 786432 | tf_op jit(solution)/shard_map/psum | solution.py:106
  146.2 18.0 %all_gather.9 = bf16[1024,128]{1,0:T(8,128)(2,1)} all-gather(bf16[64,128]{1,0:T(8,128)(2,1)S(1)} %fusion.21), channel_id=1, replica_groups=mesh['group'=8,'sub'=16] {'sub'}, dimensions={0}, use_global_device_ids=true | all-gather | bytes 278528 | tf_op jit(solution)/shard_map/all_gather | solution.py:111
  165.8 27.7 %collective-permute-start.4 = (f32[1,1,1024,128]{2,3,1,0:T(8,128)S(1)}, f32[1,1,1024,128]{2,3,1,0:T(8,128)S(1)}, u32[]{:S(2)}, u32[]{:S(2)}) collective-permute-start(f32[1,1,1024,128]{2,3,1,0:T(8,128)S(1)} %bitcast.401), channel_id=1, source_target_pairs={{0,16},{16,32},{32,48},{48,64},{64,80},{80,96},{96,112},{1,17},{17... | collective-permute-start | bytes 1572872 | tf_op jit(solution)/shard_map/ppermute | solution.py:14
  222.3 14.5 collective-permute-done.7
  298.6 15.6 collective-permute-done.11
  335.6 149.4 %all-reduce.18.cloned.1.call-done = (f32[128,128]{0,1:T(8,128)}, f32[128,128]{0,1:T(8,128)}) async-done(((f32[128,128]{0,1:T(8,128)}, f32[128,128]{0,1:T(8,128)}), (f32[128,128]{0,1:T(8,128)}, f32[128,128]{0,1:T(8,128)})) %all-reduce.18.cloned.1.call-update) | async-done | bytes 131088 | tf_op jit(solution)/shard_map/psum | solution.py:63
  488.4 12.5 cholesky.89
  502.3 9.8 custom-call.73
  518.9 64.9 %all-reduce.20 = bf16[1024,128]{1,0:T(8,128)(2,1)} all-reduce(f32[1024,128]{1,0:T(8,128)} %fusion.80), channel_id=1, replica_groups=mesh['group'=8,'sub'=16] {'sub'}, use_global_device_ids=true, to_apply=%region_9.13 | all-reduce | flops 131072 | bytes 786432 | tf_op jit(solution)/shard_map/psum | solution.py:106
  584.9 18.3 %all_gather.10 = bf16[1024,128]{1,0:T(8,128)(2,1)} all-gather(bf16[64,128]{1,0:T(8,128)(2,1)S(1)} %fusion.22), channel_id=1, replica_groups=mesh['group'=8,'sub'=16] {'sub'}, dimensions={0}, use_global_device_ids=true | all-gather | bytes 278528 | tf_op jit(solution)/shard_map/all_gather | solution.py:111
  605.6 21.6 %collective-permute-start.12 = (f32[1,1,1024,128]{2,3,1,0:T(8,128)}, f32[1,1,1024,128]{2,3,1,0:T(8,128)S(1)}, u32[]{:S(2)}, u32[]{:S(2)}) collective-permute-start(f32[1,1,1024,128]{2,3,1,0:T(8,128)} %bitcast.405), channel_id=1, source_target_pairs={{0,16},{16,32},{32,48},{48,64},{64,80},{80,96},{96,112},{1,17},{17... | collective-permute-start | bytes 1572872 | tf_op jit(solution)/shard_map/ppermute | solution.py:14
  647.9 12.5 cholesky.100
  699.7 9.8 custom-call.75
  709.5 135.7 %all-reduce.10.cloned.1.call-done = f32[128,128]{0,1:T(8,128)} async-done(((f32[128,128]{0,1:T(8,128)}), f32[128,128]{0,1:T(8,128)}) %all-reduce.10.cloned.1.call-update) | async-done | bytes 65552 | tf_op jit(solution)/shard_map/psum | solution.py:63
  882.4 13.5 collective-permute-done.19
  911.8 8.3 scatter_custom_fusion.5
  923.4 144.1 %all-reduce.12.cloned.1.call-done = f32[128,128]{0,1:T(8,128)} async-done(((f32[128,128]{0,1:T(8,128)}), f32[128,128]{0,1:T(8,128)}) %all-reduce.12.cloned.1.call-update) | async-done | bytes 65552 | tf_op jit(solution)/shard_map/psum | solution.py:63
  1070.6 13.2 cholesky.111
  1087.4 11.3 custom-call.77
  1107.0 64.4 %all-reduce.21 = bf16[1024,128]{1,0:T(8,128)(2,1)} all-reduce(f32[1024,128]{1,0:T(8,128)} %fusion.79), channel_id=1, replica_groups=mesh['group'=8,'sub'=16] {'sub'}, use_global_device_ids=true, to_apply=%region_14.18 | all-reduce | flops 131072 | bytes 786432 | tf_op jit(solution)/shard_map/psum | solution.py:106
  1172.4 18.2 %all_gather.11 = bf16[1024,128]{1,0:T(8,128)(2,1)} all-gather(bf16[64,128]{1,0:T(8,128)(2,1)S(1)} %fusion.23), channel_id=1, replica_groups=mesh['group'=8,'sub'=16] {'sub'}, dimensions={0}, use_global_device_ids=true | all-gather | bytes 278528 | tf_op jit(solution)/shard_map/all_gather | solution.py:111
  1193.0 21.2 %collective-permute-start.20 = (f32[1,1,1024,128]{2,3,1,0:T(8,128)}, f32[1,1,1024,128]{2,3,1,0:T(8,128)S(1)}, u32[]{:S(2)}, u32[]{:S(2)}) collective-permute-start(f32[1,1,1024,128]{2,3,1,0:T(8,128)} %bitcast.397), channel_id=1, source_target_pairs={{0,16},{16,32},{32,48},{48,64},{64,80},{80,96},{96,112},{1,17},{17... | collective-permute-start | bytes 1572872 | tf_op jit(solution)/shard_map/ppermute | solution.py:14
  1233.2 11.7 cholesky.122
  1274.6 8.2 scatter_custom_fusion.6
  1286.7 9.8 custom-call.79
  1296.5 134.3 %all-reduce.14.cloned.1.call-done = f32[128,128]{1,0:T(8,128)} async-done(((f32[128,128]{1,0:T(8,128)}), f32[128,128]{1,0:T(8,128)}) %all-reduce.14.cloned.1.call-update) | async-done | bytes 65552 | tf_op jit(solution)/shard_map/psum | solution.py:63
  1464.9 16.9 %collective-permute-done.27 = f32[3,1,1024,128]{2,3,1,0:T(8,128)} collective-permute-done((f32[3,1,1024,128]{2,3,1,0:T(8,128)}, f32[3,1,1024,128]{2,3,1,0:T(8,128)}, u32[]{:S(2)}, u32[]{:S(2)}) %collective-permute-start.27) | collective-permute-done | bytes 1572896 | tf_op jit(solution)/shard_map/ppermute | solution.py:14
  1494.4 8.5 scatter_custom_fusion.7
  1508.2 142.2 %all-reduce.16.cloned.1.call-done = f32[128,128]{0,1:T(8,128)} async-done(((f32[128,128]{0,1:T(8,128)}), f32[128,128]{0,1:T(8,128)}) %all-reduce.16.cloned.1.call-update) | async-done | bytes 65552 | tf_op jit(solution)/shard_map/psum | solution.py:63
  1652.2 11.7 cholesky.133
  1665.2 9.8 custom-call.81
  (313 shorter events, 432.7 us)
Async XLA Ops:
  7.2 477.8 %all-reduce.18.cloned.1.call-start = ((), (), s32[]{:S(2)}) async-start(), calls=%async_computation.4 | async-start | bytes 262144 | tf_op jit(solution)/shard_map/psum | solution.py:63
  9.2 10.9 collective-permute-start
  13.7 10.8 collective-permute-start.1
  26.9 31.5 %collective-permute-start.3 = (f32[3,1,1024,128]{3,2,1,0:T(8,128)}, f32[3,1,1024,128]{3,2,1,0:T(8,128)}, u32[]{:S(2)}, u32[]{:S(2)}) collective-permute-start(f32[3,1,1024,128]{3,2,1,0:T(8,128)} %pad_maximum_fusion), channel_id=1, source_target_pairs={{0,1},{1,2},{2,3},{3,4},{4,5},{5,6},{6,7},{7,8},{8,9},{9,10},{10,1... | collective-permute-start | bytes 4718600 | tf_op jit(solution)/shard_map/ppermute | solution.py:14
  31.3 32.4 %collective-permute-start.2 = (f32[3,1,1024,128]{3,2,1,0:T(8,128)}, f32[3,1,1024,128]{3,2,1,0:T(8,128)}, u32[]{:S(2)}, u32[]{:S(2)}) collective-permute-start(f32[3,1,1024,128]{3,2,1,0:T(8,128)} %pad_maximum_fusion), channel_id=1, source_target_pairs={{1,0},{2,1},{3,2},{4,3},{5,4},{6,5},{7,6},{8,7},{9,8},{10,9},{11,1... | collective-permute-start | bytes 4718600 | tf_op jit(solution)/shard_map/ppermute | solution.py:17
  165.8 33.9 %collective-permute-start.4 = (f32[1,1,1024,128]{2,3,1,0:T(8,128)S(1)}, f32[1,1,1024,128]{2,3,1,0:T(8,128)S(1)}, u32[]{:S(2)}, u32[]{:S(2)}) collective-permute-start(f32[1,1,1024,128]{2,3,1,0:T(8,128)S(1)} %bitcast.401), channel_id=1, source_target_pairs={{0,16},{16,32},{32,48},{48,64},{64,80},{80,96},{96,112},{1,17},{17... | collective-permute-start | bytes 1572872 | tf_op jit(solution)/shard_map/ppermute | solution.py:14
  193.6 10.5 collective-permute-start.5
  205.4 31.3 %collective-permute-start.7 = (f32[3,1,1024,128]{2,3,1,0:T(8,128)}, f32[3,1,1024,128]{2,3,1,0:T(8,128)}, u32[]{:S(2)}, u32[]{:S(2)}) collective-permute-start(f32[3,1,1024,128]{2,3,1,0:T(8,128)} %pad_maximum_fusion.1), channel_id=1, source_target_pairs={{0,1},{1,2},{2,3},{3,4},{4,5},{5,6},{6,7},{7,8},{8,9},{9,10},{10,1... | collective-permute-start | bytes 4718600 | tf_op jit(solution)/shard_map/ppermute | solution.py:14
  210.0 33.7 %collective-permute-start.6 = (f32[3,1,1024,128]{2,3,1,0:T(8,128)}, f32[3,1,1024,128]{2,3,1,0:T(8,128)}, u32[]{:S(2)}, u32[]{:S(2)}) collective-permute-start(f32[3,1,1024,128]{2,3,1,0:T(8,128)} %pad_maximum_fusion.1), channel_id=1, source_target_pairs={{1,0},{2,1},{3,2},{4,3},{5,4},{6,5},{7,6},{8,7},{9,8},{10,9},{11,1... | collective-permute-start | bytes 4718600 | tf_op jit(solution)/shard_map/ppermute | solution.py:17
  261.9 14.2 collective-permute-start.8
  269.9 10.5 collective-permute-start.9
  281.8 32.4 %collective-permute-start.11 = (f32[3,1,1024,128]{2,3,1,0:T(8,128)}, f32[3,1,1024,128]{2,3,1,0:T(8,128)}, u32[]{:S(2)}, u32[]{:S(2)}) collective-permute-start(f32[3,1,1024,128]{2,3,1,0:T(8,128)} %pad_maximum_fusion.2), channel_id=1, source_target_pairs={{0,1},{1,2},{2,3},{3,4},{4,5},{5,6},{6,7},{7,8},{8,9},{9,10},{10,1... | collective-permute-start | bytes 4718600 | tf_op jit(solution)/shard_map/ppermute | solution.py:14
  287.5 32.0 %collective-permute-start.10 = (f32[3,1,1024,128]{2,3,1,0:T(8,128)}, f32[3,1,1024,128]{2,3,1,0:T(8,128)}, u32[]{:S(2)}, u32[]{:S(2)}) collective-permute-start(f32[3,1,1024,128]{2,3,1,0:T(8,128)} %pad_maximum_fusion.2), channel_id=1, source_target_pairs={{1,0},{2,1},{3,2},{4,3},{5,4},{6,5},{7,6},{8,7},{9,8},{10,9},{11,1... | collective-permute-start | bytes 4718600 | tf_op jit(solution)/shard_map/ppermute | solution.py:17
  335.5 509.6 %all-reduce.10.cloned.1.call-start = ((), (), s32[]{:S(2)}) async-start(), calls=%async_computation | async-start | bytes 131072 | tf_op jit(solution)/shard_map/psum | solution.py:63
  605.6 28.0 %collective-permute-start.12 = (f32[1,1,1024,128]{2,3,1,0:T(8,128)}, f32[1,1,1024,128]{2,3,1,0:T(8,128)S(1)}, u32[]{:S(2)}, u32[]{:S(2)}) collective-permute-start(f32[1,1,1024,128]{2,3,1,0:T(8,128)} %bitcast.405), channel_id=1, source_target_pairs={{0,16},{16,32},{32,48},{48,64},{64,80},{80,96},{96,112},{1,17},{17... | collective-permute-start | bytes 1572872 | tf_op jit(solution)/shard_map/ppermute | solution.py:14
  627.1 10.7 collective-permute-start.13
  640.4 31.3 %collective-permute-start.15 = (f32[3,1,1024,128]{2,3,1,0:T(8,128)}, f32[3,1,1024,128]{2,3,1,0:T(8,128)}, u32[]{:S(2)}, u32[]{:S(2)}) collective-permute-start(f32[3,1,1024,128]{2,3,1,0:T(8,128)} %pad_maximum_fusion.3), channel_id=1, source_target_pairs={{0,1},{1,2},{2,3},{3,4},{4,5},{5,6},{6,7},{7,8},{8,9},{9,10},{10,1... | collective-permute-start | bytes 4718600 | tf_op jit(solution)/shard_map/ppermute | solution.py:14
  644.6 34.0 %collective-permute-start.14 = (f32[3,1,1024,128]{2,3,1,0:T(8,128)}, f32[3,1,1024,128]{2,3,1,0:T(8,128)}, u32[]{:S(2)}, u32[]{:S(2)}) collective-permute-start(f32[3,1,1024,128]{2,3,1,0:T(8,128)} %pad_maximum_fusion.3), channel_id=1, source_target_pairs={{1,0},{2,1},{3,2},{4,3},{5,4},{6,5},{7,6},{8,7},{9,8},{10,9},{11,1... | collective-permute-start | bytes 4718600 | tf_op jit(solution)/shard_map/ppermute | solution.py:17
  698.7 368.8 %all-reduce.12.cloned.1.call-start = ((), (), s32[]{:S(2)}) async-start(), calls=%async_computation.1 | async-start | bytes 131072 | tf_op jit(solution)/shard_map/psum | solution.py:63
  850.5 8.5 collective-permute-start.16
  853.0 10.5 collective-permute-start.17
  864.8 31.1 %collective-permute-start.19 = (f32[3,1,1024,128]{2,3,1,0:T(8,128)}, f32[3,1,1024,128]{2,3,1,0:T(8,128)}, u32[]{:S(2)}, u32[]{:S(2)}) collective-permute-start(f32[3,1,1024,128]{2,3,1,0:T(8,128)} %pad_maximum_fusion.4), channel_id=1, source_target_pairs={{0,1},{1,2},{2,3},{3,4},{4,5},{5,6},{6,7},{7,8},{8,9},{9,10},{10,1... | collective-permute-start | bytes 4718600 | tf_op jit(solution)/shard_map/ppermute | solution.py:14
  868.9 33.9 %collective-permute-start.18 = (f32[3,1,1024,128]{2,3,1,0:T(8,128)}, f32[3,1,1024,128]{2,3,1,0:T(8,128)}, u32[]{:S(2)}, u32[]{:S(2)}) collective-permute-start(f32[3,1,1024,128]{2,3,1,0:T(8,128)} %pad_maximum_fusion.4), channel_id=1, source_target_pairs={{1,0},{2,1},{3,2},{4,3},{5,4},{6,5},{7,6},{8,7},{9,8},{10,9},{11,1... | collective-permute-start | bytes 4718600 | tf_op jit(solution)/shard_map/ppermute | solution.py:17
  922.9 507.9 %all-reduce.14.cloned.1.call-start = ((), (), s32[]{:S(2)}) async-start(), calls=%async_computation.2 | async-start | bytes 131072 | tf_op jit(solution)/shard_map/psum | solution.py:63
  1193.0 27.6 %collective-permute-start.20 = (f32[1,1,1024,128]{2,3,1,0:T(8,128)}, f32[1,1,1024,128]{2,3,1,0:T(8,128)S(1)}, u32[]{:S(2)}, u32[]{:S(2)}) collective-permute-start(f32[1,1,1024,128]{2,3,1,0:T(8,128)} %bitcast.397), channel_id=1, source_target_pairs={{0,16},{16,32},{32,48},{48,64},{64,80},{80,96},{96,112},{1,17},{17... | collective-permute-start | bytes 1572872 | tf_op jit(solution)/shard_map/ppermute | solution.py:14
  1214.2 10.7 collective-permute-start.21
  1227.4 31.3 %collective-permute-start.23 = (f32[3,1,1024,128]{2,3,1,0:T(8,128)}, f32[3,1,1024,128]{2,3,1,0:T(8,128)}, u32[]{:S(2)}, u32[]{:S(2)}) collective-permute-start(f32[3,1,1024,128]{2,3,1,0:T(8,128)} %pad_maximum_fusion.5), channel_id=1, source_target_pairs={{0,1},{1,2},{2,3},{3,4},{4,5},{5,6},{6,7},{7,8},{8,9},{9,10},{10,1... | collective-permute-start | bytes 4718600 | tf_op jit(solution)/shard_map/ppermute | solution.py:14
  1231.6 34.0 %collective-permute-start.22 = (f32[3,1,1024,128]{2,3,1,0:T(8,128)}, f32[3,1,1024,128]{2,3,1,0:T(8,128)}, u32[]{:S(2)}, u32[]{:S(2)}) collective-permute-start(f32[3,1,1024,128]{2,3,1,0:T(8,128)} %pad_maximum_fusion.5), channel_id=1, source_target_pairs={{1,0},{2,1},{3,2},{4,3},{5,4},{6,5},{7,6},{8,7},{9,8},{10,9},{11,1... | collective-permute-start | bytes 4718600 | tf_op jit(solution)/shard_map/ppermute | solution.py:17
  1285.8 364.6 %all-reduce.16.cloned.1.call-start = ((), (), s32[]{:S(2)}) async-start(), calls=%async_computation.3 | async-start | bytes 131072 | tf_op jit(solution)/shard_map/psum | solution.py:63
  1438.9 10.5 collective-permute-start.25
  1450.7 31.1 %collective-permute-start.27 = (f32[3,1,1024,128]{2,3,1,0:T(8,128)}, f32[3,1,1024,128]{2,3,1,0:T(8,128)}, u32[]{:S(2)}, u32[]{:S(2)}) collective-permute-start(f32[3,1,1024,128]{2,3,1,0:T(8,128)} %pad_maximum_fusion.6), channel_id=1, source_target_pairs={{0,1},{1,2},{2,3},{3,4},{4,5},{5,6},{6,7},{7,8},{8,9},{9,10},{10,1... | collective-permute-start | bytes 4718600 | tf_op jit(solution)/shard_map/ppermute | solution.py:14
  1454.9 32.2 %collective-permute-start.26 = (f32[3,1,1024,128]{2,3,1,0:T(8,128)}, f32[3,1,1024,128]{2,3,1,0:T(8,128)}, u32[]{:S(2)}, u32[]{:S(2)}) collective-permute-start(f32[3,1,1024,128]{2,3,1,0:T(8,128)} %pad_maximum_fusion.6), channel_id=1, source_target_pairs={{1,0},{2,1},{3,2},{4,3},{5,4},{6,5},{7,6},{8,7},{9,8},{10,9},{11,1... | collective-permute-start | bytes 4718600 | tf_op jit(solution)/shard_map/ppermute | solution.py:17
  (35 other events, 1593.9 us)
Sparse Core Ops, SparseCore 0:
  335.7 149.2 all-reduce.17
  698.8 146.3 all-reduce.9
  923.0 144.4 all-reduce.11
  1285.9 144.8 all-reduce.13
  1505.9 144.4 all-reduce.15
where the time goes:
time: 1700 us; the launch traced here: 1690 us
  waiting for transfers between devices  842 us (50%)
  blocking collectives  250 us (15%)
  other arithmetic  218 us (13%)
  local copies, waits for them, and re-layouts  155 us (9%)
  starting transfers between devices  143 us (8%)
  matrix products  63.4 us (4%)
    psum x5, waiting for transfers between devices, gram_matrix(): return lax.psum(local_gram, ('group', 'sub'))  706 us
    psum x3, blocking collectives, precondition(): coarse_residual = lax.psum(contrib, 'sub')  196 us
    ppermute x14, starting transfers between devices, extended(): lax.ppermute(lax.slice_in_dim(block, block.shape[dim] - width, None, axis...  119 us
    ppermute x14, waiting for transfers between devices, extended(): lax.ppermute(lax.slice_in_dim(block, block.shape[dim] - width, None, axis...  103 us
    gather x28, local copies, waits for them, and re-layouts, pick_rows(): source_block[rows_at]  70.6 us
    another operation x15, other arithmetic, spd_solve(): factor = jnp.linalg.cholesky(matrix)  66 us
    another operation x10, other arithmetic, spd_solve(): lax.linalg.triangular_solve(factor, half, left_side=True, lower=True, tra...  55.3 us
    all_gather x3, blocking collectives, precondition(): coarse_values = lax.all_gather(row_values, 'sub', axis=0, tiled=True)  54.4 us
  transfers between devices with their start and end apart: 33, of which 27 were waited for; matrix products, arithmetic and copies ran while one was open for 10% of the time, Pallas kernels for 0%

commit v1 on v0

--- a/solution.py
+++ b/solution.py
@@ -60,7 +60,7 @@
     local_gram = jnp.einsum(
         "gsir,gsic->rc", left * weight[..., None], right, precision=lax.Precision.HIGHEST
     )
-    return lax.psum(local_gram, ("group", "sub"))
+    return lax.psum(lax.psum(local_gram, "group"), "sub")
 
 
 def spd_solve(matrix, rhs_block):

time: 1700 us -> 1730 us (1.018)
    psum x5 -> x10, waiting for transfers between devices: 706 us -> 717 us  [gram_matrix(): return lax.psum(lax.psum(local_gram, 'group'), 'sub')]
  transfers between devices with their start and end apart: 33 -> 38, of which waited for: 27 -> 32; matrix products, arithmetic and copies ran while one was open for 10% -> 10% of each run, Pallas kernels for 0% -> 0%
where the time goes in v1:
time: 1730 us; the launch traced here: 1720 us
  waiting for transfers between devices  851 us (49%)
  blocking collectives  251 us (15%)
  other arithmetic  217 us (13%)
  local copies, waits for them, and re-layouts  162 us (9%)
  starting transfers between devices  156 us (9%)
  matrix products  63.5 us (4%)
    psum x10, waiting for transfers between devices, gram_matrix(): return lax.psum(lax.psum(local_gram, 'group'), 'sub')  717 us
    psum x3, blocking collectives, precondition(): coarse_residual = lax.psum(contrib, 'sub')  197 us
    ppermute x14, starting transfers between devices, extended(): lax.ppermute(lax.slice_in_dim(block, block.shape[dim] - width, None, axis...  132 us
    ppermute x14, waiting for transfers between devices, extended(): lax.ppermute(lax.slice_in_dim(block, block.shape[dim] - width, None, axis...  101 us
    gather x28, local copies, waits for them, and re-layouts, pick_rows(): source_block[rows_at]  75 us
    another operation x15, other arithmetic, spd_solve(): factor = jnp.linalg.cholesky(matrix)  65.9 us
    another operation x10, other arithmetic, spd_solve(): lax.linalg.triangular_solve(factor, half, left_side=True, lower=True, tra...  55 us
    all_gather x3, blocking collectives, precondition(): coarse_values = lax.all_gather(row_values, 'sub', axis=0, tiled=True)  54.3 us
  transfers between devices with their start and end apart: 38, of which 32 were waited for; matrix products, arithmetic and copies ran while one was open for 10% of the time, Pallas kernels for 0%

profile of v1, /device:TPU:1, one launch (start us, length us, event | category | flops | bytes accessed | tf_op | source)
XLA Modules:
  0.0 1717.0 jit_solution(1084324587988879409)
XLA Ops:
  44.1 14.3 collective-permute-done.3
  78.4 66.6 %all-reduce.35 = bf16[1024,128]{1,0:T(8,128)(2,1)} all-reduce(f32[1024,128]{1,0:T(8,128)S(1)} %fusion.81), channel_id=1, replica_groups=mesh['group'=8,'sub'=16] {'sub'}, use_global_device_ids=true, to_apply=%region_2.0 | all-reduce | flops 131072 | bytes 786432 | tf_op jit(solution)/shard_map/psum | solution.py:106
  146.2 18.0 %all_gather.9 = bf16[1024,128]{1,0:T(8,128)(2,1)} all-gather(bf16[64,128]{1,0:T(8,128)(2,1)S(1)} %fusion.21), channel_id=1, replica_groups=mesh['group'=8,'sub'=16] {'sub'}, dimensions={0}, use_global_device_ids=true | all-gather | bytes 278528 | tf_op jit(solution)/shard_map/all_gather | solution.py:111
  165.8 27.8 %collective-permute-start.4 = (f32[1,1,1024,128]{2,3,1,0:T(8,128)S(1)}, f32[1,1,1024,128]{2,3,1,0:T(8,128)S(1)}, u32[]{:S(2)}, u32[]{:S(2)}) collective-permute-start(f32[1,1,1024,128]{2,3,1,0:T(8,128)S(1)} %bitcast.401), channel_id=1, source_target_pairs={{0,16},{16,32},{32,48},{48,64},{64,80},{80,96},{96,112},{1,17},{17... | collective-permute-start | bytes 1572872 | tf_op jit(solution)/shard_map/ppermute | solution.py:14
  222.3 14.5 collective-permute-done.7
  298.6 15.7 collective-permute-done.11
  335.6 64.9 %all-reduce.34.cloned.1.call-done = (f32[128,128]{0,1:T(8,128)}, f32[128,128]{0,1:T(8,128)}) async-done(((f32[128,128]{0,1:T(8,128)}, f32[128,128]{0,1:T(8,128)}), (f32[128,128]{0,1:T(8,128)}, f32[128,128]{0,1:T(8,128)})) %all-reduce.34.cloned.1.call-update) | async-done | bytes 131088 | tf_op jit(solution)/shard_map/psum | solution.py:63
  400.6 86.1 %all-reduce.32.cloned.1.call-done = (f32[128,128]{0,1:T(8,128)}, f32[128,128]{0,1:T(8,128)}) async-done(((f32[128,128]{0,1:T(8,128)}, f32[128,128]{0,1:T(8,128)}), (f32[128,128]{0,1:T(8,128)}, f32[128,128]{0,1:T(8,128)})) %all-reduce.32.cloned.1.call-update) | async-done | bytes 131088 | tf_op jit(solution)/shard_map/psum | solution.py:63
  490.1 12.5 cholesky.89
  504.0 9.8 custom-call.73
  520.6 65.2 %all-reduce.36 = bf16[1024,128]{1,0:T(8,128)(2,1)} all-reduce(f32[1024,128]{1,0:T(8,128)} %fusion.80), channel_id=1, replica_groups=mesh['group'=8,'sub'=16] {'sub'}, use_global_device_ids=true, to_apply=%region_11.15 | all-reduce | flops 131072 | bytes 786432 | tf_op jit(solution)/shard_map/psum | solution.py:106
  586.9 18.3 %all_gather.10 = bf16[1024,128]{1,0:T(8,128)(2,1)} all-gather(bf16[64,128]{1,0:T(8,128)(2,1)S(1)} %fusion.22), channel_id=1, replica_groups=mesh['group'=8,'sub'=16] {'sub'}, dimensions={0}, use_global_device_ids=true | all-gather | bytes 278528 | tf_op jit(solution)/shard_map/all_gather | solution.py:111
  607.7 24.1 %collective-permute-start.12 = (f32[1,1,1024,128]{2,3,1,0:T(8,128)}, f32[1,1,1024,128]{2,3,1,0:T(8,128)S(1)}, u32[]{:S(2)}, u32[]{:S(2)}) collective-permute-start(f32[1,1,1024,128]{2,3,1,0:T(8,128)} %bitcast.405), channel_id=1, source_target_pairs={{0,16},{16,32},{32,48},{48,64},{64,80},{80,96},{96,112},{1,17},{17... | collective-permute-start | bytes 1572872 | tf_op jit(solution)/shard_map/ppermute | solution.py:14
  652.5 12.5 cholesky.100
  704.0 63.2 %all-reduce.16.cloned.1.call-done = f32[128,128]{0,1:T(8,128)} async-done(((f32[128,128]{0,1:T(8,128)}), f32[128,128]{0,1:T(8,128)}) %all-reduce.16.cloned.1.call-update) | async-done | bytes 65552 | tf_op jit(solution)/shard_map/psum | solution.py:63
  768.1 9.8 custom-call.75
  777.9 73.9 %all-reduce.18.cloned.1.call-done = f32[128,128]{0,1:T(8,128)} async-done(((f32[128,128]{0,1:T(8,128)}), f32[128,128]{0,1:T(8,128)}) %all-reduce.18.cloned.1.call-update) | async-done | bytes 65552 | tf_op jit(solution)/shard_map/psum | solution.py:63
  892.3 13.3 collective-permute-done.19
  932.6 63.6 %all-reduce.20.cloned.1.call-done = f32[128,128]{0,1:T(8,128)} async-done(((f32[128,128]{0,1:T(8,128)}), f32[128,128]{0,1:T(8,128)}) %all-reduce.20.cloned.1.call-update) | async-done | bytes 65552 | tf_op jit(solution)/shard_map/psum | solution.py:63
  996.7 84.0 %all-reduce.22.cloned.1.call-done = f32[128,128]{0,1:T(8,128)} async-done(((f32[128,128]{0,1:T(8,128)}), f32[128,128]{0,1:T(8,128)}) %all-reduce.22.cloned.1.call-update) | async-done | bytes 65552 | tf_op jit(solution)/shard_map/psum | solution.py:63
  1083.8 13.2 cholesky.111
  1100.6 11.3 custom-call.77
  1120.1 64.8 %all-reduce.37 = bf16[1024,128]{1,0:T(8,128)(2,1)} all-reduce(f32[1024,128]{1,0:T(8,128)} %fusion.79), channel_id=1, replica_groups=mesh['group'=8,'sub'=16] {'sub'}, use_global_device_ids=true, to_apply=%region_18.22 | all-reduce | flops 131072 | bytes 786432 | tf_op jit(solution)/shard_map/psum | solution.py:106
  1186.0 18.0 %all_gather.11 = bf16[1024,128]{1,0:T(8,128)(2,1)} all-gather(bf16[64,128]{1,0:T(8,128)(2,1)S(1)} %fusion.23), channel_id=1, replica_groups=mesh['group'=8,'sub'=16] {'sub'}, dimensions={0}, use_global_device_ids=true | all-gather | bytes 278528 | tf_op jit(solution)/shard_map/all_gather | solution.py:111
  1206.4 24.6 %collective-permute-start.20 = (f32[1,1,1024,128]{2,3,1,0:T(8,128)}, f32[1,1,1024,128]{2,3,1,0:T(8,128)S(1)}, u32[]{:S(2)}, u32[]{:S(2)}) collective-permute-start(f32[1,1,1024,128]{2,3,1,0:T(8,128)} %bitcast.397), channel_id=1, source_target_pairs={{0,16},{16,32},{32,48},{48,64},{64,80},{80,96},{96,112},{1,17},{17... | collective-permute-start | bytes 1572872 | tf_op jit(solution)/shard_map/ppermute | solution.py:14
  1250.0 11.7 cholesky.122
  1303.3 63.2 %all-reduce.24.cloned.1.call-done = f32[128,128]{1,0:T(8,128)} async-done(((f32[128,128]{1,0:T(8,128)}), f32[128,128]{1,0:T(8,128)}) %all-reduce.24.cloned.1.call-update) | async-done | bytes 65552 | tf_op jit(solution)/shard_map/psum | solution.py:63
  1377.2 74.0 %all-reduce.26.cloned.1.call-done = f32[128,128]{1,0:T(8,128)} async-done(((f32[128,128]{1,0:T(8,128)}), f32[128,128]{1,0:T(8,128)}) %all-reduce.26.cloned.1.call-update) | async-done | bytes 65552 | tf_op jit(solution)/shard_map/psum | solution.py:63
  1491.3 13.9 collective-permute-done.27
  1534.2 62.0 %all-reduce.28.cloned.1.call-done = f32[128,128]{0,1:T(8,128)} async-done(((f32[128,128]{0,1:T(8,128)}), f32[128,128]{0,1:T(8,128)}) %all-reduce.28.cloned.1.call-update) | async-done | bytes 65552 | tf_op jit(solution)/shard_map/psum | solution.py:63
  1598.6 82.1 %all-reduce.30.cloned.1.call-done = f32[128,128]{0,1:T(8,128)} async-done(((f32[128,128]{0,1:T(8,128)}), f32[128,128]{0,1:T(8,128)}) %all-reduce.30.cloned.1.call-update) | async-done | bytes 65552 | tf_op jit(solution)/shard_map/psum | solution.py:63
  1682.5 11.7 cholesky.133
  (326 shorter events, 492.8 us)
Async XLA Ops:
  7.2 393.3 %all-reduce.34.cloned.1.call-start = ((), (), s32[]{:S(2)}) async-start(), calls=%async_computation.9 | async-start | bytes 262144 | tf_op jit(solution)/shard_map/psum | solution.py:63
  9.2 10.9 collective-permute-start
  13.7 10.8 collective-permute-start.1
  26.9 31.5 %collective-permute-start.3 = (f32[3,1,1024,128]{3,2,1,0:T(8,128)}, f32[3,1,1024,128]{3,2,1,0:T(8,128)}, u32[]{:S(2)}, u32[]{:S(2)}) collective-permute-start(f32[3,1,1024,128]{3,2,1,0:T(8,128)} %pad_maximum_fusion), channel_id=1, source_target_pairs={{0,1},{1,2},{2,3},{3,4},{4,5},{5,6},{6,7},{7,8},{8,9},{9,10},{10,1... | collective-permute-start | bytes 4718600 | tf_op jit(solution)/shard_map/ppermute | solution.py:14
  31.3 32.4 %collective-permute-start.2 = (f32[3,1,1024,128]{3,2,1,0:T(8,128)}, f32[3,1,1024,128]{3,2,1,0:T(8,128)}, u32[]{:S(2)}, u32[]{:S(2)}) collective-permute-start(f32[3,1,1024,128]{3,2,1,0:T(8,128)} %pad_maximum_fusion), channel_id=1, source_target_pairs={{1,0},{2,1},{3,2},{4,3},{5,4},{6,5},{7,6},{8,7},{9,8},{10,9},{11,1... | collective-permute-start | bytes 4718600 | tf_op jit(solution)/shard_map/ppermute | solution.py:17
  165.8 33.9 %collective-permute-start.4 = (f32[1,1,1024,128]{2,3,1,0:T(8,128)S(1)}, f32[1,1,1024,128]{2,3,1,0:T(8,128)S(1)}, u32[]{:S(2)}, u32[]{:S(2)}) collective-permute-start(f32[1,1,1024,128]{2,3,1,0:T(8,128)S(1)} %bitcast.401), channel_id=1, source_target_pairs={{0,16},{16,32},{32,48},{48,64},{64,80},{80,96},{96,112},{1,17},{17... | collective-permute-start | bytes 1572872 | tf_op jit(solution)/shard_map/ppermute | solution.py:14
  205.4 31.3 %collective-permute-start.7 = (f32[3,1,1024,128]{2,3,1,0:T(8,128)}, f32[3,1,1024,128]{2,3,1,0:T(8,128)}, u32[]{:S(2)}, u32[]{:S(2)}) collective-permute-start(f32[3,1,1024,128]{2,3,1,0:T(8,128)} %pad_maximum_fusion.1), channel_id=1, source_target_pairs={{0,1},{1,2},{2,3},{3,4},{4,5},{5,6},{6,7},{7,8},{8,9},{9,10},{10,1... | collective-permute-start | bytes 4718600 | tf_op jit(solution)/shard_map/ppermute | solution.py:14
  210.0 33.7 %collective-permute-start.6 = (f32[3,1,1024,128]{2,3,1,0:T(8,128)}, f32[3,1,1024,128]{2,3,1,0:T(8,128)}, u32[]{:S(2)}, u32[]{:S(2)}) collective-permute-start(f32[3,1,1024,128]{2,3,1,0:T(8,128)} %pad_maximum_fusion.1), channel_id=1, source_target_pairs={{1,0},{2,1},{3,2},{4,3},{5,4},{6,5},{7,6},{8,7},{9,8},{10,9},{11,1... | collective-permute-start | bytes 4718600 | tf_op jit(solution)/shard_map/ppermute | solution.py:17
  261.9 14.2 collective-permute-start.8
  281.8 32.4 %collective-permute-start.11 = (f32[3,1,1024,128]{2,3,1,0:T(8,128)}, f32[3,1,1024,128]{2,3,1,0:T(8,128)}, u32[]{:S(2)}, u32[]{:S(2)}) collective-permute-start(f32[3,1,1024,128]{2,3,1,0:T(8,128)} %pad_maximum_fusion.2), channel_id=1, source_target_pairs={{0,1},{1,2},{2,3},{3,4},{4,5},{5,6},{6,7},{7,8},{8,9},{9,10},{10,1... | collective-permute-start | bytes 4718600 | tf_op jit(solution)/shard_map/ppermute | solution.py:14
  287.5 32.0 %collective-permute-start.10 = (f32[3,1,1024,128]{2,3,1,0:T(8,128)}, f32[3,1,1024,128]{2,3,1,0:T(8,128)}, u32[]{:S(2)}, u32[]{:S(2)}) collective-permute-start(f32[3,1,1024,128]{2,3,1,0:T(8,128)} %pad_maximum_fusion.2), channel_id=1, source_target_pairs={{1,0},{2,1},{3,2},{4,3},{5,4},{6,5},{7,6},{8,7},{9,8},{10,9},{11,1... | collective-permute-start | bytes 4718600 | tf_op jit(solution)/shard_map/ppermute | solution.py:17
  335.6 151.2 %all-reduce.32.cloned.1.call-start = ((), (), s32[]{:S(2)}) async-start(), calls=%async_computation.8 | async-start | bytes 262144 | tf_op jit(solution)/shard_map/psum | solution.py:63
  400.5 366.7 %all-reduce.16.cloned.1.call-start = ((), (), s32[]{:S(2)}) async-start(), calls=%async_computation | async-start | bytes 131072 | tf_op jit(solution)/shard_map/psum | solution.py:63
  607.7 30.5 %collective-permute-start.12 = (f32[1,1,1024,128]{2,3,1,0:T(8,128)}, f32[1,1,1024,128]{2,3,1,0:T(8,128)S(1)}, u32[]{:S(2)}, u32[]{:S(2)}) collective-permute-start(f32[1,1,1024,128]{2,3,1,0:T(8,128)} %bitcast.405), channel_id=1, source_target_pairs={{0,16},{16,32},{32,48},{48,64},{64,80},{80,96},{96,112},{1,17},{17... | collective-permute-start | bytes 1572872 | tf_op jit(solution)/shard_map/ppermute | solution.py:14
  645.0 31.3 %collective-permute-start.15 = (f32[3,1,1024,128]{2,3,1,0:T(8,128)}, f32[3,1,1024,128]{2,3,1,0:T(8,128)}, u32[]{:S(2)}, u32[]{:S(2)}) collective-permute-start(f32[3,1,1024,128]{2,3,1,0:T(8,128)} %pad_maximum_fusion.3), channel_id=1, source_target_pairs={{0,1},{1,2},{2,3},{3,4},{4,5},{5,6},{6,7},{7,8},{8,9},{9,10},{10,1... | collective-permute-start | bytes 4718600 | tf_op jit(solution)/shard_map/ppermute | solution.py:14
  649.2 34.0 %collective-permute-start.14 = (f32[3,1,1024,128]{2,3,1,0:T(8,128)}, f32[3,1,1024,128]{2,3,1,0:T(8,128)}, u32[]{:S(2)}, u32[]{:S(2)}) collective-permute-start(f32[3,1,1024,128]{2,3,1,0:T(8,128)} %pad_maximum_fusion.3), channel_id=1, source_target_pairs={{1,0},{2,1},{3,2},{4,3},{5,4},{6,5},{7,6},{8,7},{9,8},{10,9},{11,1... | collective-permute-start | bytes 4718600 | tf_op jit(solution)/shard_map/ppermute | solution.py:17
  703.3 148.5 %all-reduce.18.cloned.1.call-start = ((), (), s32[]{:S(2)}) async-start(), calls=%async_computation.1 | async-start | bytes 131072 | tf_op jit(solution)/shard_map/psum | solution.py:63
  767.2 229.0 %all-reduce.20.cloned.1.call-start = ((), (), s32[]{:S(2)}) async-start(), calls=%async_computation.2 | async-start | bytes 131072 | tf_op jit(solution)/shard_map/psum | solution.py:63
  857.2 11.5 collective-permute-start.16
  874.4 31.1 %collective-permute-start.19 = (f32[3,1,1024,128]{2,3,1,0:T(8,128)}, f32[3,1,1024,128]{2,3,1,0:T(8,128)}, u32[]{:S(2)}, u32[]{:S(2)}) collective-permute-start(f32[3,1,1024,128]{2,3,1,0:T(8,128)} %pad_maximum_fusion.4), channel_id=1, source_target_pairs={{0,1},{1,2},{2,3},{3,4},{4,5},{5,6},{6,7},{7,8},{8,9},{9,10},{10,1... | collective-permute-start | bytes 4718600 | tf_op jit(solution)/shard_map/ppermute | solution.py:14
  878.8 33.6 %collective-permute-start.18 = (f32[3,1,1024,128]{2,3,1,0:T(8,128)}, f32[3,1,1024,128]{2,3,1,0:T(8,128)}, u32[]{:S(2)}, u32[]{:S(2)}) collective-permute-start(f32[3,1,1024,128]{2,3,1,0:T(8,128)} %pad_maximum_fusion.4), channel_id=1, source_target_pairs={{1,0},{2,1},{3,2},{4,3},{5,4},{6,5},{7,6},{8,7},{9,8},{10,9},{11,1... | collective-permute-start | bytes 4718600 | tf_op jit(solution)/shard_map/ppermute | solution.py:17
  932.5 148.2 %all-reduce.22.cloned.1.call-start = ((), (), s32[]{:S(2)}) async-start(), calls=%async_computation.3 | async-start | bytes 131072 | tf_op jit(solution)/shard_map/psum | solution.py:63
  996.2 370.2 %all-reduce.24.cloned.1.call-start = ((), (), s32[]{:S(2)}) async-start(), calls=%async_computation.4 | async-start | bytes 131072 | tf_op jit(solution)/shard_map/psum | solution.py:63
  1206.4 31.0 %collective-permute-start.20 = (f32[1,1,1024,128]{2,3,1,0:T(8,128)}, f32[1,1,1024,128]{2,3,1,0:T(8,128)S(1)}, u32[]{:S(2)}, u32[]{:S(2)}) collective-permute-start(f32[1,1,1024,128]{2,3,1,0:T(8,128)} %bitcast.397), channel_id=1, source_target_pairs={{0,16},{16,32},{32,48},{48,64},{64,80},{80,96},{96,112},{1,17},{17... | collective-permute-start | bytes 1572872 | tf_op jit(solution)/shard_map/ppermute | solution.py:14
  1244.2 31.3 %collective-permute-start.23 = (f32[3,1,1024,128]{2,3,1,0:T(8,128)}, f32[3,1,1024,128]{2,3,1,0:T(8,128)}, u32[]{:S(2)}, u32[]{:S(2)}) collective-permute-start(f32[3,1,1024,128]{2,3,1,0:T(8,128)} %pad_maximum_fusion.5), channel_id=1, source_target_pairs={{0,1},{1,2},{2,3},{3,4},{4,5},{5,6},{6,7},{7,8},{8,9},{9,10},{10,1... | collective-permute-start | bytes 4718600 | tf_op jit(solution)/shard_map/ppermute | solution.py:14
  1248.4 34.0 %collective-permute-start.22 = (f32[3,1,1024,128]{2,3,1,0:T(8,128)}, f32[3,1,1024,128]{2,3,1,0:T(8,128)}, u32[]{:S(2)}, u32[]{:S(2)}) collective-permute-start(f32[3,1,1024,128]{2,3,1,0:T(8,128)} %pad_maximum_fusion.5), channel_id=1, source_target_pairs={{1,0},{2,1},{3,2},{4,3},{5,4},{6,5},{7,6},{8,7},{9,8},{10,9},{11,1... | collective-permute-start | bytes 4718600 | tf_op jit(solution)/shard_map/ppermute | solution.py:17
  1302.6 148.6 %all-reduce.26.cloned.1.call-start = ((), (), s32[]{:S(2)}) async-start(), calls=%async_computation.5 | async-start | bytes 131072 | tf_op jit(solution)/shard_map/psum | solution.py:63
  1366.5 229.7 %all-reduce.28.cloned.1.call-start = ((), (), s32[]{:S(2)}) async-start(), calls=%async_computation.6 | async-start | bytes 131072 | tf_op jit(solution)/shard_map/psum | solution.py:63
  1456.8 11.5 collective-permute-start.24
  1474.1 31.1 %collective-permute-start.27 = (f32[3,1,1024,128]{2,3,1,0:T(8,128)}, f32[3,1,1024,128]{2,3,1,0:T(8,128)}, u32[]{:S(2)}, u32[]{:S(2)}) collective-permute-start(f32[3,1,1024,128]{2,3,1,0:T(8,128)} %pad_maximum_fusion.6), channel_id=1, source_target_pairs={{0,1},{1,2},{2,3},{3,4},{4,5},{5,6},{6,7},{7,8},{8,9},{9,10},{10,1... | collective-permute-start | bytes 4718600 | tf_op jit(solution)/shard_map/ppermute | solution.py:14
  1478.5 33.7 %collective-permute-start.26 = (f32[3,1,1024,128]{2,3,1,0:T(8,128)}, f32[3,1,1024,128]{2,3,1,0:T(8,128)}, u32[]{:S(2)}, u32[]{:S(2)}) collective-permute-start(f32[3,1,1024,128]{2,3,1,0:T(8,128)} %pad_maximum_fusion.6), channel_id=1, source_target_pairs={{1,0},{2,1},{3,2},{4,3},{5,4},{6,5},{7,6},{8,7},{9,8},{10,9},{11,1... | collective-permute-start | bytes 4718600 | tf_op jit(solution)/shard_map/ppermute | solution.py:17
  1532.5 148.2 %all-reduce.30.cloned.1.call-start = ((), (), s32[]{:S(2)}) async-start(), calls=%async_computation.7 | async-start | bytes 131072 | tf_op jit(solution)/shard_map/psum | solution.py:63
  (39 other events, 1657.5 us)
Sparse Core Ops, SparseCore 0:
  335.7 64.7 all-reduce.33
  403.8 82.8 all-reduce.31
  703.4 63.7 all-reduce.15
  770.2 81.4 all-reduce.17
  932.6 63.5 all-reduce.19
  999.3 81.4 all-reduce.21
  1302.7 63.6 all-reduce.23
  1369.7 81.4 all-reduce.25
  1532.6 63.5 all-reduce.27
  1599.2 81.4 all-reduce.29
